TPU v7x, 32 devices: a whole 2x2x4 slice. The times are simulated.
32 devices in a mesh: wide: 8 (over z, x), narrow: 4 (over y, core).
Axes of the slice: x: 2, y: 2, z: 4, core: 2. Of those that a mesh axis runs over, the one named last changes fastest.
Arguments:
- embeddings: bfloat16 [8192, 512], P(('wide', 'narrow')), may hold values from -26 to 26
- partners: int32 [32, 7], P(('wide', 'narrow')), may hold values from -1 to 7, as said below
- pair_kind: int32 [32, 7], P(('wide', 'narrow')), may hold values from 0 to 1, as said below
- neighbors: int32 [7, 15, 8192], P(None, None, ('wide', 'narrow')), may hold values from 0 to 255
Outputs:
- gradient: float32 [8192, 512], P(('wide', 'narrow'))
- mean_loss: float32 [], replicated
Inputs may be any that keep to these rules, and one draw needn't show every extreme that they name: Row w * 4 + n lists the wide indices of that block's partners in ascending order, then -1 in the remaining slots; a partner has the same narrow index n, is never the block itself, appears once, and the pairing is mutual. In every narrow index one block is paired with all 7 others. `pair_kind`: 1 marks a graph pair, 0 a sampled negative or an empty slot; both directions of a pair carry the same mark, and every block has at least one graph pair.
All inputs are finite; a program needn't handle non-finite values.
Results may differ from a plain program's by a relative error of at most 0.0004.
Values may be sent and summed in bfloat16 or wider, within the bound.
No kernel may reach another device: no remote copies, remote signals or barrier semaphores. Data moves between devices by JAX's collectives and lax.ppermute only.
A program may use at most 64 MiB of HBM per device.

v0:
```python
import jax
import jax.numpy as jnp
from jax import lax
from jax.sharding import PartitionSpec as P


def tile_kernel(local_rows, remote_rows, local_norms, features):
    remote_norms = jnp.sum(jnp.square(remote_rows.astype(jnp.float32)), axis=1)
    inner = jnp.einsum("id,jd->ij", local_rows, remote_rows, preferred_element_type=jnp.float32)
    distance = local_norms[:, None] + remote_norms[None, :] - 2.0 * inner
    return 1.0 / (1.0 + distance / features)


def edge_counts(targets, block_rows):
    columns = lax.broadcasted_iota(jnp.int32, (1, 1, block_rows), 2)
    return jnp.sum((targets[:, :, None] == columns).astype(jnp.float32), axis=0)


def mirrored_counts(sources, block_rows):
    rows_index = lax.broadcasted_iota(jnp.int32, (1, block_rows, 1), 1)
    return jnp.sum((sources[:, None, :] == rows_index).astype(jnp.float32), axis=0)


def per_device(embeddings, partners, pair_kind, neighbors):
    block_rows, features = embeddings.shape
    slot_count = partners.shape[1]
    groups = lax.axis_size("wide")
    column = lax.all_gather(embeddings, "wide", axis=0, tiled=True).reshape(
        groups, block_rows, features
    )
    local_float = embeddings.astype(jnp.float32)
    local_norms = jnp.sum(jnp.square(local_float), axis=1)
    partner_row = partners[0]
    mark_row = pair_kind[0].astype(jnp.float32)

    def remote_of(slot):
        partner = partner_row[slot]
        return (
            partner,
            lax.dynamic_index_in_dim(column, jnp.maximum(partner, 0), 0, keepdims=False),
        )

    def first(slot, carry):

        def first_active(carry):
            sums, kernels, counts_store = carry
            partner, remote_rows = remote_of(slot)
            kernel = tile_kernel(embeddings, remote_rows, local_norms, features)
            targets = lax.dynamic_index_in_dim(neighbors, slot, 0, keepdims=False)
            counts = edge_counts(targets, block_rows) * mark_row[slot]
            sums = (
                sums[0] + jnp.sum(kernel),
                sums[1] + jnp.sum(counts * jnp.log(kernel)),
                sums[2] + jnp.sum(counts),
                sums[3] + float(block_rows * block_rows),
            )
            kernels = lax.dynamic_update_index_in_dim(kernels, kernel, slot, 0)
            counts_store = lax.dynamic_update_index_in_dim(counts_store, counts, slot, 0)
            return (sums, kernels, counts_store)

        return lax.cond(partner_row[slot] >= 0, first_active, lambda carry: carry, carry)

    nothing = jnp.zeros((), jnp.float32)
    empty_tiles = jnp.zeros((slot_count, block_rows, block_rows), jnp.float32)
    sums, kernels, counts_store = lax.fori_loop(
        0, slot_count, first, ((nothing, nothing, nothing, nothing), empty_tiles, empty_tiles)
    )
    kernel_sum, attract_sum, edge_sum, entry_sum = sums
    total, attract, edges_total, entries = lax.psum(
        (kernel_sum, attract_sum, edge_sum, entry_sum), ("wide", "narrow")
    )
    mean_loss = -attract / edges_total + jnp.log(total / entries)
    repulsion = edges_total / total
    start_gradient = jnp.zeros((block_rows, features), jnp.float32)
    selector = (partner_row[None, :] == lax.broadcasted_iota(jnp.int32, (groups, 1), 0)).astype(
        jnp.int32
    )
    outgoing = jnp.tensordot(selector, neighbors, axes=1)
    incoming = lax.all_to_all(outgoing, "wide", split_axis=0, concat_axis=0, tiled=True)

    def second(slot, gradient):

        def second_active(gradient):
            partner, remote_rows = remote_of(slot)
            kernel = lax.dynamic_index_in_dim(kernels, slot, 0, keepdims=False)
            counts = lax.dynamic_index_in_dim(counts_store, slot, 0, keepdims=False)
            sources = lax.dynamic_index_in_dim(incoming, jnp.maximum(partner, 0), 0, keepdims=False)
            back_counts = mirrored_counts(sources, block_rows) * mark_row[slot]
            weight = (counts * kernel - repulsion * kernel * kernel) / features
            mirror = (back_counts * kernel - repulsion * kernel * kernel) / features
            row_total = jnp.sum(weight, axis=1) + jnp.sum(mirror, axis=1)
            product = jnp.dot(
                weight.astype(jnp.bfloat16), remote_rows, preferred_element_type=jnp.float32
            ) + jnp.dot(
                mirror.astype(jnp.bfloat16), remote_rows, preferred_element_type=jnp.float32
            )
            return gradient + 2.0 * (row_total[:, None] * local_float - product)

        return lax.cond(partner_row[slot] >= 0, second_active, lambda gradient: gradient, gradient)

    gradient = lax.fori_loop(0, slot_count, second, start_gradient)
    return (gradient, mean_loss)


def solution(mesh):
    in_specs = (
        P(("wide", "narrow"), None),
        P(("wide", "narrow"), None),
        P(("wide", "narrow"), None),
        P(None, None, ("wide", "narrow")),
    )
    out_specs = (P(("wide", "narrow"), None), P())
    return jax.shard_map(
        per_device, mesh=mesh, in_specs=in_specs, out_specs=out_specs, check_vma=False
    )
```

profile of v0, /device:TPU:0, one launch (start us, length us, event | category | flops | bytes accessed | tf_op | source)
XLA Modules:
  0.0 261.6 jit_solution(13438871651944459247)
XLA Ops:
  9.8 7.3 %all-to-all-start = ((s32[8,15,256]{2,1,0:T(8,128)}), s32[8,15,256]{2,1,0:T(8,128)S(1)}, u32[]{:S(2)}, u32[]{:S(2)}) async-start(s32[8,15,256]{2,1,0:T(8,128)} %copy.16), calls=%async_computation | async-start | bytes 262144 | tf_op jit(solution)/shard_map/all_to_all | solution.py:79
  18.2 43.7 %all-gather.2.cloned.1.call-done = bf16[2048,512]{1,0:T(8,128)(2,1)} async-done(((bf16[256,512]{1,0:T(8,128)(2,1)}), bf16[2048,512]{1,0:T(8,128)(2,1)}) %all-gather.2.cloned.1.call-update) | async-done | bytes 2097168 | tf_op jit(solution)/shard_map/all_gather | solution.py:28
  63.5 80.1 %while.39 = (s32[]{:T(128)}, f32[]{:T(128)}, f32[]{:T(128)}, f32[]{:T(128)}, f32[]{:T(128)}, /*index=5*/f32[7,256,256]{1,2,0:T(8,128)S(1)}, f32[7,256,256]{1,2,0...) while((s32[]{:T(128)}, f32[]{:T(128)}, f32[]{:T(128)}, ...), condition=%wide.region_9.10_spmd, body=%wide.region_1.9_spmd.sunk | while | flops 71171840 | bytes 3196933 | solution.py:65
  64.8 10.2 %conditional.4 = ((f32[]{:T(128)}, f32[]{:T(128)}, f32[]{:T(128)}, f32[]{:T(128)}, f32[7,256,256]{1,2,0:T(8,128)S(1)}, /*index=5*/f32[7,256,256]{1,2,0:T(8,128)})) conditional(s32[]{:T(128)} %bitcast.84, (f32[]{:T(128)}, f32[]{:T(128)}, f32[]{:T(128)}, f32[]{:T(128)}, f32[7,256,256]{1,2,0:T(8,128)S(1)}, ...), branch_computations={%region_2.0_spmd, %region_3.8_spmd} | conditional | flops 71171840 | bytes 3196614 | solution.py:61
  69.3 2.6 multiply_reduce_fusion.2
  76.2 10.2 %conditional.4 = ((f32[]{:T(128)}, f32[]{:T(128)}, f32[]{:T(128)}, f32[]{:T(128)}, f32[7,256,256]{1,2,0:T(8,128)S(1)}, /*index=5*/f32[7,256,256]{1,2,0:T(8,128)})) conditional(s32[]{:T(128)} %bitcast.84, (f32[]{:T(128)}, f32[]{:T(128)}, f32[]{:T(128)}, f32[]{:T(128)}, f32[7,256,256]{1,2,0:T(8,128)S(1)}, ...), branch_computations={%region_2.0_spmd, %region_3.8_spmd} | conditional | flops 71171840 | bytes 3196614 | solution.py:61
  87.6 10.2 %conditional.4 = ((f32[]{:T(128)}, f32[]{:T(128)}, f32[]{:T(128)}, f32[]{:T(128)}, f32[7,256,256]{1,2,0:T(8,128)S(1)}, /*index=5*/f32[7,256,256]{1,2,0:T(8,128)})) conditional(s32[]{:T(128)} %bitcast.84, (f32[]{:T(128)}, f32[]{:T(128)}, f32[]{:T(128)}, f32[]{:T(128)}, f32[7,256,256]{1,2,0:T(8,128)S(1)}, ...), branch_computations={%region_2.0_spmd, %region_3.8_spmd} | conditional | flops 71171840 | bytes 3196614 | solution.py:61
  99.1 10.2 %conditional.4 = ((f32[]{:T(128)}, f32[]{:T(128)}, f32[]{:T(128)}, f32[]{:T(128)}, f32[7,256,256]{1,2,0:T(8,128)S(1)}, /*index=5*/f32[7,256,256]{1,2,0:T(8,128)})) conditional(s32[]{:T(128)} %bitcast.84, (f32[]{:T(128)}, f32[]{:T(128)}, f32[]{:T(128)}, f32[]{:T(128)}, f32[7,256,256]{1,2,0:T(8,128)S(1)}, ...), branch_computations={%region_2.0_spmd, %region_3.8_spmd} | conditional | flops 71171840 | bytes 3196614 | solution.py:61
  103.6 2.5 multiply_reduce_fusion.2
  110.5 10.2 %conditional.4 = ((f32[]{:T(128)}, f32[]{:T(128)}, f32[]{:T(128)}, f32[]{:T(128)}, f32[7,256,256]{1,2,0:T(8,128)S(1)}, /*index=5*/f32[7,256,256]{1,2,0:T(8,128)})) conditional(s32[]{:T(128)} %bitcast.84, (f32[]{:T(128)}, f32[]{:T(128)}, f32[]{:T(128)}, f32[]{:T(128)}, f32[7,256,256]{1,2,0:T(8,128)S(1)}, ...), branch_computations={%region_2.0_spmd, %region_3.8_spmd} | conditional | flops 71171840 | bytes 3196614 | solution.py:61
  122.0 10.2 %conditional.4 = ((f32[]{:T(128)}, f32[]{:T(128)}, f32[]{:T(128)}, f32[]{:T(128)}, f32[7,256,256]{1,2,0:T(8,128)S(1)}, /*index=5*/f32[7,256,256]{1,2,0:T(8,128)})) conditional(s32[]{:T(128)} %bitcast.84, (f32[]{:T(128)}, f32[]{:T(128)}, f32[]{:T(128)}, f32[]{:T(128)}, f32[7,256,256]{1,2,0:T(8,128)S(1)}, ...), branch_computations={%region_2.0_spmd, %region_3.8_spmd} | conditional | flops 71171840 | bytes 3196614 | solution.py:61
  126.5 2.6 multiply_reduce_fusion.2
  133.4 10.2 %conditional.4 = ((f32[]{:T(128)}, f32[]{:T(128)}, f32[]{:T(128)}, f32[]{:T(128)}, f32[7,256,256]{1,2,0:T(8,128)S(1)}, /*index=5*/f32[7,256,256]{1,2,0:T(8,128)})) conditional(s32[]{:T(128)} %bitcast.84, (f32[]{:T(128)}, f32[]{:T(128)}, f32[]{:T(128)}, f32[]{:T(128)}, f32[7,256,256]{1,2,0:T(8,128)S(1)}, ...), branch_computations={%region_2.0_spmd, %region_3.8_spmd} | conditional | flops 71171840 | bytes 3196614 | solution.py:61
  137.9 2.5 multiply_reduce_fusion.2
  143.6 41.4 %all-reduce = (f32[]{:T(128)}, f32[]{:T(128)}, f32[]{:T(128)}, f32[]{:T(128)}) all-reduce(f32[]{:T(128)} %get-tuple-element.499, f32[]{:T(128)} %get-tuple-element.500, f32[]{:T(128)} %get-tuple-element.502, f32[]{:T(128)} %get-tuple-element.503), channel_id=1, replica_groups=mesh['wide'=8,'narrow'=4] {'wide','narrow'}, use_global_device_ids=true, to_apply=%region_10.11 | all-reduce | flops 4 | bytes 32 | tf_op jit(solution)/shard_map/psum | solution.py:69
  189.0 2.7 %copy.17 = f32[7,256,256]{2,1,0:T(8,128)} copy(f32[7,256,256]{1,2,0:T(8,128)} %get-tuple-element.527) | data formatting | bytes 3670016 | tf_op jit(solution)/shard_map/while | solution.py:101
  193.6 59.2 %while.40 = (s32[]{:T(128)}, f32[256,512]{1,0:T(8,128)S(1)}, s32[7]{0:T(128)S(1)}, f32[7,256,256]{2,1,0:T(8,128)}, f32[7,256,256]{2,1,0:T(8,128)S(1)}, /*index=5...) while((s32[]{:T(128)}, f32[256,512]{1,0:T(8,128)S(1)}, ...), condition=%wide.region_18.19_spmd, body=%wide.region_12.18_spmd.sunk | while | flops 139329280 | bytes 5297989 | solution.py:101
  194.9 7.2 %conditional.5 = (f32[256,512]{1,0:T(8,128)S(1)}) conditional(s32[]{:T(128)} %bitcast.85, f32[256,512]{1,0:T(8,128)S(1)} %get-tuple-element.814, (s32[]{:T(128)}, f32[7,256,256]{2,1,0:T(8,128)}, f32[7,256,256]{2,1,0:T(8,128)S(1)}, f32[]{:T(128)}, s32[7]{0:T(128)S(1)}, /*index=5*/s32[8,15,256]{2,1,0:T(8,128)S(1)}, f32[7]{0:T(128)S(1)}, ...), branch_computations={%region_13.13_spmd, %region_14.17_spmd} | conditional | flops 139329280 | bytes 5297766 | solution.py:99
  203.3 7.2 %conditional.5 = (f32[256,512]{1,0:T(8,128)S(1)}) conditional(s32[]{:T(128)} %bitcast.85, f32[256,512]{1,0:T(8,128)S(1)} %get-tuple-element.814, (s32[]{:T(128)}, f32[7,256,256]{2,1,0:T(8,128)}, f32[7,256,256]{2,1,0:T(8,128)S(1)}, f32[]{:T(128)}, s32[7]{0:T(128)S(1)}, /*index=5*/s32[8,15,256]{2,1,0:T(8,128)S(1)}, f32[7]{0:T(128)S(1)}, ...), branch_computations={%region_13.13_spmd, %region_14.17_spmd} | conditional | flops 139329280 | bytes 5297766 | solution.py:99
  211.8 7.2 %conditional.5 = (f32[256,512]{1,0:T(8,128)S(1)}) conditional(s32[]{:T(128)} %bitcast.85, f32[256,512]{1,0:T(8,128)S(1)} %get-tuple-element.814, (s32[]{:T(128)}, f32[7,256,256]{2,1,0:T(8,128)}, f32[7,256,256]{2,1,0:T(8,128)S(1)}, f32[]{:T(128)}, s32[7]{0:T(128)S(1)}, /*index=5*/s32[8,15,256]{2,1,0:T(8,128)S(1)}, f32[7]{0:T(128)S(1)}, ...), branch_computations={%region_13.13_spmd, %region_14.17_spmd} | conditional | flops 139329280 | bytes 5297766 | solution.py:99
  220.3 7.2 %conditional.5 = (f32[256,512]{1,0:T(8,128)S(1)}) conditional(s32[]{:T(128)} %bitcast.85, f32[256,512]{1,0:T(8,128)S(1)} %get-tuple-element.814, (s32[]{:T(128)}, f32[7,256,256]{2,1,0:T(8,128)}, f32[7,256,256]{2,1,0:T(8,128)S(1)}, f32[]{:T(128)}, s32[7]{0:T(128)S(1)}, /*index=5*/s32[8,15,256]{2,1,0:T(8,128)S(1)}, f32[7]{0:T(128)S(1)}, ...), branch_computations={%region_13.13_spmd, %region_14.17_spmd} | conditional | flops 139329280 | bytes 5297766 | solution.py:99
  228.7 7.2 %conditional.5 = (f32[256,512]{1,0:T(8,128)S(1)}) conditional(s32[]{:T(128)} %bitcast.85, f32[256,512]{1,0:T(8,128)S(1)} %get-tuple-element.814, (s32[]{:T(128)}, f32[7,256,256]{2,1,0:T(8,128)}, f32[7,256,256]{2,1,0:T(8,128)S(1)}, f32[]{:T(128)}, s32[7]{0:T(128)S(1)}, /*index=5*/s32[8,15,256]{2,1,0:T(8,128)S(1)}, f32[7]{0:T(128)S(1)}, ...), branch_computations={%region_13.13_spmd, %region_14.17_spmd} | conditional | flops 139329280 | bytes 5297766 | solution.py:99
  237.2 7.2 %conditional.5 = (f32[256,512]{1,0:T(8,128)S(1)}) conditional(s32[]{:T(128)} %bitcast.85, f32[256,512]{1,0:T(8,128)S(1)} %get-tuple-element.814, (s32[]{:T(128)}, f32[7,256,256]{2,1,0:T(8,128)}, f32[7,256,256]{2,1,0:T(8,128)S(1)}, f32[]{:T(128)}, s32[7]{0:T(128)S(1)}, /*index=5*/s32[8,15,256]{2,1,0:T(8,128)S(1)}, f32[7]{0:T(128)S(1)}, ...), branch_computations={%region_13.13_spmd, %region_14.17_spmd} | conditional | flops 139329280 | bytes 5297766 | solution.py:99
  245.6 7.2 %conditional.5 = (f32[256,512]{1,0:T(8,128)S(1)}) conditional(s32[]{:T(128)} %bitcast.85, f32[256,512]{1,0:T(8,128)S(1)} %get-tuple-element.814, (s32[]{:T(128)}, f32[7,256,256]{2,1,0:T(8,128)}, f32[7,256,256]{2,1,0:T(8,128)S(1)}, f32[]{:T(128)}, s32[7]{0:T(128)S(1)}, /*index=5*/s32[8,15,256]{2,1,0:T(8,128)S(1)}, f32[7]{0:T(128)S(1)}, ...), branch_computations={%region_13.13_spmd, %region_14.17_spmd} | conditional | flops 139329280 | bytes 5297766 | solution.py:99
  (144 shorter events, 106.4 us)
Async XLA Ops:
  7.2 10.9 %copy-start.2 = (bf16[256,512]{1,0:T(8,128)(2,1)S(1)}, bf16[256,512]{1,0:T(8,128)(2,1)}, u32[]{:S(2)}) copy-start(bf16[256,512]{1,0:T(8,128)(2,1)} %param.12) | copy-start | bytes 786436
  7.2 11.0 %copy-start.4 = (s32[1,7]{1,0:T(1,128)S(1)}, s32[1,7]{1,0:T(1,128)}, u32[]{:S(2)}) copy-start(s32[1,7]{1,0:T(1,128)} %param.14) | copy-start | bytes 88
  7.2 54.8 %all-gather.2.cloned.1.call-start = ((), (), s32[]{:S(2)}) async-start(), calls=%async_computation.1 | async-start | bytes 2359296 | tf_op jit(solution)/shard_map/all_gather | solution.py:28
  9.8 183.8 %all-to-all-start = ((s32[8,15,256]{2,1,0:T(8,128)}), s32[8,15,256]{2,1,0:T(8,128)S(1)}, u32[]{:S(2)}, u32[]{:S(2)}) async-start(s32[8,15,256]{2,1,0:T(8,128)} %copy.16), calls=%async_computation | async-start | bytes 262144 | tf_op jit(solution)/shard_map/all_to_all | solution.py:79
  62.0 1.6 copy-start.3
  143.6 48.1 %copy-start.1 = (f32[7,256,256]{1,2,0:T(8,128)}, f32[7,256,256]{1,2,0:T(8,128)S(1)}, u32[]{:S(2)}) copy-start(f32[7,256,256]{1,2,0:T(8,128)S(1)} %get-tuple-element.528) | copy-start | bytes 5505028
  252.9 0.8 copy-start
Sparse Core Ops, SparseCore 0:
  10.1 51.8 all-gather.1
where the time goes:
time: 264 us; the launch traced here: 262 us
  waiting for transfers between devices  44.4 us (17%)
  blocking collectives  41.4 us (16%)
  matrix products  40.6 us (15%)
  other arithmetic  39.2 us (15%)
  local copies, waits for them, and re-layouts  38.7 us (15%)
  loops' own time  30.7 us (12%)
  between operations  19.2 us (7%)
  starting transfers between devices  7.32 us (3%)
    all_gather x1, waiting for transfers between devices, per_device(): lax.all_gather(embeddings, 'wide', axis=0, tiled=True)  43.7 us
    psum x1, blocking collectives, per_device(): lax.psum((kernel_sum, attract_sum, edge_sum, entry_sum), ('wide', 'narrow'))  41.4 us
    dot_general x7, matrix products, tile_kernel(): jnp.einsum('id,jd->ij', local_rows, remote_rows, preferred_element_type=j...  17.8 us
    another operation x7, loops' own time, first(): lax.cond(partner_row[slot] >= 0, first_active, lambda carry: carry, carry)  16.8 us
    dot_general x7, matrix products, second_active(): jnp.dot(mirror.astype(jnp.bfloat16), remote_rows, preferred_element_type=...  12.8 us
    reduce_sum x7, other arithmetic, second_active(): row_total = jnp.sum(weight, axis=1) + jnp.sum(mirror, axis=1)  12.2 us
    dynamic_update_slice x7, other arithmetic, first_active(): lax.dynamic_update_index_in_dim(counts_store, counts, slot, 0)  9.57 us
    dot_general x7, matrix products, second_active(): jnp.dot(weight.astype(jnp.bfloat16), remote_rows, preferred_element_type=...  8.86 us
  transfers between devices with their start and end apart: 2, of which 1 were waited for; matrix products, arithmetic and copies ran while one was open for 26% of the time, Pallas kernels for 0%

commit v1 on v0

--- a/solution.py
+++ b/solution.py
@@ -67,7 +67,7 @@
     )
     kernel_sum, attract_sum, edge_sum, entry_sum = sums
     total, attract, edges_total, entries = lax.psum(
-        (kernel_sum, attract_sum, edge_sum, entry_sum), ("wide", "narrow")
+        lax.psum((kernel_sum, attract_sum, edge_sum, entry_sum), "narrow"), "wide"
     )
     mean_loss = -attract / edges_total + jnp.log(total / entries)
     repulsion = edges_total / total

time: 264 us -> 249 us (0.943)
  blocking collectives: 41.4 us -> 26.5 us
    psum x1 -> x2, blocking collectives: 41.4 us -> 26.5 us  [the longest x1 17.8 us: per_device(): lax.psum(lax.psum((kernel_sum, attract_sum, edge_sum, entry_sum), 'narrow...]
  transfers between devices with their start and end apart: 2 -> 2, of which waited for: 1 -> 1; matrix products, arithmetic and copies ran while one was open for 26% -> 28% of each run, Pallas kernels for 0% -> 0%
where the time goes in v1:
time: 249 us; the launch traced here: 247 us
  waiting for transfers between devices  44.4 us (18%)
  matrix products  40.6 us (16%)
  other arithmetic  39.2 us (16%)
  local copies, waits for them, and re-layouts  38.7 us (16%)
  loops' own time  30.7 us (12%)
  blocking collectives  26.5 us (11%)
  between operations  19.1 us (8%)
  starting transfers between devices  7.32 us (3%)
    all_gather x1, waiting for transfers between devices, per_device(): lax.all_gather(embeddings, 'wide', axis=0, tiled=True)  43.7 us
    dot_general x7, matrix products, tile_kernel(): jnp.einsum('id,jd->ij', local_rows, remote_rows, preferred_element_type=j...  17.8 us
    psum x1, blocking collectives, per_device(): lax.psum(lax.psum((kernel_sum, attract_sum, edge_sum, entry_sum), 'narrow...  17.8 us
    another operation x7, loops' own time, first(): lax.cond(partner_row[slot] >= 0, first_active, lambda carry: carry, carry)  16.8 us
    dot_general x7, matrix products, second_active(): jnp.dot(mirror.astype(jnp.bfloat16), remote_rows, preferred_element_type=...  12.8 us
    reduce_sum x7, other arithmetic, second_active(): row_total = jnp.sum(weight, axis=1) + jnp.sum(mirror, axis=1)  12.2 us
    dynamic_update_slice x7, other arithmetic, first_active(): lax.dynamic_update_index_in_dim(counts_store, counts, slot, 0)  9.57 us
    dot_general x7, matrix products, second_active(): jnp.dot(weight.astype(jnp.bfloat16), remote_rows, preferred_element_type=...  8.86 us
  transfers between devices with their start and end apart: 2, of which 1 were waited for; matrix products, arithmetic and copies ran while one was open for 28% of the time, Pallas kernels for 0%

profile of v1, /device:TPU:0, one launch (start us, length us, event | category | flops | bytes accessed | tf_op | source)
XLA Modules:
  0.0 246.6 jit_solution(12889111559476052318)
XLA Ops:
  9.8 7.3 %all-to-all-start = ((s32[8,15,256]{2,1,0:T(8,128)}), s32[8,15,256]{2,1,0:T(8,128)S(1)}, u32[]{:S(2)}, u32[]{:S(2)}) async-start(s32[8,15,256]{2,1,0:T(8,128)} %copy.16), calls=%async_computation | async-start | bytes 262144 | tf_op jit(solution)/shard_map/all_to_all | solution.py:79
  18.2 43.7 %all-gather.2.cloned.1.call-done = bf16[2048,512]{1,0:T(8,128)(2,1)} async-done(((bf16[256,512]{1,0:T(8,128)(2,1)}), bf16[2048,512]{1,0:T(8,128)(2,1)}) %all-gather.2.cloned.1.call-update) | async-done | bytes 2097168 | tf_op jit(solution)/shard_map/all_gather | solution.py:28
  63.5 80.1 %while.39 = (s32[]{:T(128)}, f32[]{:T(128)}, f32[]{:T(128)}, f32[]{:T(128)}, f32[]{:T(128)}, /*index=5*/f32[7,256,256]{1,2,0:T(8,128)S(1)}, f32[7,256,256]{1,2,0...) while((s32[]{:T(128)}, f32[]{:T(128)}, f32[]{:T(128)}, ...), condition=%wide.region_9.10_spmd, body=%wide.region_1.9_spmd.sunk | while | flops 71171840 | bytes 3196933 | solution.py:65
  64.8 10.2 %conditional.4 = ((f32[]{:T(128)}, f32[]{:T(128)}, f32[]{:T(128)}, f32[]{:T(128)}, f32[7,256,256]{1,2,0:T(8,128)S(1)}, /*index=5*/f32[7,256,256]{1,2,0:T(8,128)})) conditional(s32[]{:T(128)} %bitcast.84, (f32[]{:T(128)}, f32[]{:T(128)}, f32[]{:T(128)}, f32[]{:T(128)}, f32[7,256,256]{1,2,0:T(8,128)S(1)}, ...), branch_computations={%region_2.0_spmd, %region_3.8_spmd} | conditional | flops 71171840 | bytes 3196614 | solution.py:61
  69.3 2.6 %multiply_reduce_fusion.2 = (f32[]{:T(128)}, f32[]{:T(128)}, f32[]{:T(128)}, f32[256,256]{0,1:T(8,128)S(1)}) fusion(f32[256,256]{0,1:T(8,128)S(1)} %copy.14, f32[]{:T(128)} %bitcast.4, bf16[256,512]{1,0:T(8,128)(2,1)S(1)} %get-tuple-element.439, bf16[8,256,512]{2,1,0:T(8,128)(2,1)} %get-tuple-element.436, s32[]{:T(128)} %bitcast, ...), kind=kOutput, calls=%fused_computation.13 | convolution fusion | flops 67829760 | bytes 1051660 | tf_op jit(solution)/shard_map/while/body/eval_jaxpr/cond/branch_1_fun/id,jd->ij/dot_general | solution.py:9
  76.2 10.2 %conditional.4 = ((f32[]{:T(128)}, f32[]{:T(128)}, f32[]{:T(128)}, f32[]{:T(128)}, f32[7,256,256]{1,2,0:T(8,128)S(1)}, /*index=5*/f32[7,256,256]{1,2,0:T(8,128)})) conditional(s32[]{:T(128)} %bitcast.84, (f32[]{:T(128)}, f32[]{:T(128)}, f32[]{:T(128)}, f32[]{:T(128)}, f32[7,256,256]{1,2,0:T(8,128)S(1)}, ...), branch_computations={%region_2.0_spmd, %region_3.8_spmd} | conditional | flops 71171840 | bytes 3196614 | solution.py:61
  87.6 10.2 %conditional.4 = ((f32[]{:T(128)}, f32[]{:T(128)}, f32[]{:T(128)}, f32[]{:T(128)}, f32[7,256,256]{1,2,0:T(8,128)S(1)}, /*index=5*/f32[7,256,256]{1,2,0:T(8,128)})) conditional(s32[]{:T(128)} %bitcast.84, (f32[]{:T(128)}, f32[]{:T(128)}, f32[]{:T(128)}, f32[]{:T(128)}, f32[7,256,256]{1,2,0:T(8,128)S(1)}, ...), branch_computations={%region_2.0_spmd, %region_3.8_spmd} | conditional | flops 71171840 | bytes 3196614 | solution.py:61
  99.1 10.2 %conditional.4 = ((f32[]{:T(128)}, f32[]{:T(128)}, f32[]{:T(128)}, f32[]{:T(128)}, f32[7,256,256]{1,2,0:T(8,128)S(1)}, /*index=5*/f32[7,256,256]{1,2,0:T(8,128)})) conditional(s32[]{:T(128)} %bitcast.84, (f32[]{:T(128)}, f32[]{:T(128)}, f32[]{:T(128)}, f32[]{:T(128)}, f32[7,256,256]{1,2,0:T(8,128)S(1)}, ...), branch_computations={%region_2.0_spmd, %region_3.8_spmd} | conditional | flops 71171840 | bytes 3196614 | solution.py:61
  110.5 10.2 %conditional.4 = ((f32[]{:T(128)}, f32[]{:T(128)}, f32[]{:T(128)}, f32[]{:T(128)}, f32[7,256,256]{1,2,0:T(8,128)S(1)}, /*index=5*/f32[7,256,256]{1,2,0:T(8,128)})) conditional(s32[]{:T(128)} %bitcast.84, (f32[]{:T(128)}, f32[]{:T(128)}, f32[]{:T(128)}, f32[]{:T(128)}, f32[7,256,256]{1,2,0:T(8,128)S(1)}, ...), branch_computations={%region_2.0_spmd, %region_3.8_spmd} | conditional | flops 71171840 | bytes 3196614 | solution.py:61
  122.0 10.2 %conditional.4 = ((f32[]{:T(128)}, f32[]{:T(128)}, f32[]{:T(128)}, f32[]{:T(128)}, f32[7,256,256]{1,2,0:T(8,128)S(1)}, /*index=5*/f32[7,256,256]{1,2,0:T(8,128)})) conditional(s32[]{:T(128)} %bitcast.84, (f32[]{:T(128)}, f32[]{:T(128)}, f32[]{:T(128)}, f32[]{:T(128)}, f32[7,256,256]{1,2,0:T(8,128)S(1)}, ...), branch_computations={%region_2.0_spmd, %region_3.8_spmd} | conditional | flops 71171840 | bytes 3196614 | solution.py:61
  126.5 2.6 %multiply_reduce_fusion.2 = (f32[]{:T(128)}, f32[]{:T(128)}, f32[]{:T(128)}, f32[256,256]{0,1:T(8,128)S(1)}) fusion(f32[256,256]{0,1:T(8,128)S(1)} %copy.14, f32[]{:T(128)} %bitcast.4, bf16[256,512]{1,0:T(8,128)(2,1)S(1)} %get-tuple-element.439, bf16[8,256,512]{2,1,0:T(8,128)(2,1)} %get-tuple-element.436, s32[]{:T(128)} %bitcast, ...), kind=kOutput, calls=%fused_computation.13 | convolution fusion | flops 67829760 | bytes 1051660 | tf_op jit(solution)/shard_map/while/body/eval_jaxpr/cond/branch_1_fun/id,jd->ij/dot_general | solution.py:9
  133.4 10.2 %conditional.4 = ((f32[]{:T(128)}, f32[]{:T(128)}, f32[]{:T(128)}, f32[]{:T(128)}, f32[7,256,256]{1,2,0:T(8,128)S(1)}, /*index=5*/f32[7,256,256]{1,2,0:T(8,128)})) conditional(s32[]{:T(128)} %bitcast.84, (f32[]{:T(128)}, f32[]{:T(128)}, f32[]{:T(128)}, f32[]{:T(128)}, f32[7,256,256]{1,2,0:T(8,128)S(1)}, ...), branch_computations={%region_2.0_spmd, %region_3.8_spmd} | conditional | flops 71171840 | bytes 3196614 | solution.py:61
  137.9 2.5 %multiply_reduce_fusion.2 = (f32[]{:T(128)}, f32[]{:T(128)}, f32[]{:T(128)}, f32[256,256]{0,1:T(8,128)S(1)}) fusion(f32[256,256]{0,1:T(8,128)S(1)} %copy.14, f32[]{:T(128)} %bitcast.4, bf16[256,512]{1,0:T(8,128)(2,1)S(1)} %get-tuple-element.439, bf16[8,256,512]{2,1,0:T(8,128)(2,1)} %get-tuple-element.436, s32[]{:T(128)} %bitcast, ...), kind=kOutput, calls=%fused_computation.13 | convolution fusion | flops 67829760 | bytes 1051660 | tf_op jit(solution)/shard_map/while/body/eval_jaxpr/cond/branch_1_fun/id,jd->ij/dot_general | solution.py:9
  143.6 8.7 %all-reduce.1 = (f32[]{:T(128)}, f32[]{:T(128)}, f32[]{:T(128)}, f32[]{:T(128)}) all-reduce(f32[]{:T(128)} %get-tuple-element.499, f32[]{:T(128)} %get-tuple-element.500, f32[]{:T(128)} %get-tuple-element.502, f32[]{:T(128)} %get-tuple-element.503), channel_id=1, replica_groups=mesh['wide'=8,'narrow'=4] {'narrow'}, use_global_device_ids=true, to_apply=%region_10.11 | all-reduce | flops 4 | bytes 32 | tf_op jit(solution)/shard_map/psum | solution.py:70
  152.3 17.8 %all-reduce = (f32[]{:T(128)}, f32[]{:T(128)}, f32[]{:T(128)}, f32[]{:T(128)}) all-reduce(f32[]{:T(128)} %get-tuple-element.589, f32[]{:T(128)} %get-tuple-element.590, f32[]{:T(128)} %get-tuple-element.591, f32[]{:T(128)} %get-tuple-element.592), channel_id=1, replica_groups=mesh['wide'=8,'narrow'=4] {'wide'}, use_global_device_ids=true, to_apply=%region_11.12 | all-reduce | flops 4 | bytes 32 | tf_op jit(solution)/shard_map/psum | solution.py:69
  174.0 2.7 %copy.17 = f32[7,256,256]{2,1,0:T(8,128)} copy(f32[7,256,256]{1,2,0:T(8,128)} %get-tuple-element.527) | data formatting | bytes 3670016 | tf_op jit(solution)/shard_map/while | solution.py:101
  178.6 59.2 %while.40 = (s32[]{:T(128)}, f32[256,512]{1,0:T(8,128)S(1)}, s32[7]{0:T(128)S(1)}, f32[7,256,256]{2,1,0:T(8,128)}, f32[7,256,256]{2,1,0:T(8,128)S(1)}, /*index=5...) while((s32[]{:T(128)}, f32[256,512]{1,0:T(8,128)S(1)}, ...), condition=%wide.region_20.21_spmd, body=%wide.region_14.20_spmd.sunk | while | flops 139329280 | bytes 5297989 | solution.py:101
  179.9 7.2 %conditional.5 = (f32[256,512]{1,0:T(8,128)S(1)}) conditional(s32[]{:T(128)} %bitcast.85, f32[256,512]{1,0:T(8,128)S(1)} %get-tuple-element.818, (s32[]{:T(128)}, f32[7,256,256]{2,1,0:T(8,128)}, f32[7,256,256]{2,1,0:T(8,128)S(1)}, f32[]{:T(128)}, s32[7]{0:T(128)S(1)}, /*index=5*/s32[8,15,256]{2,1,0:T(8,128)S(1)}, f32[7]{0:T(128)S(1)}, ...), branch_computations={%region_15.15_spmd, %region_16.19_spmd} | conditional | flops 139329280 | bytes 5297766 | solution.py:99
  188.3 7.2 %conditional.5 = (f32[256,512]{1,0:T(8,128)S(1)}) conditional(s32[]{:T(128)} %bitcast.85, f32[256,512]{1,0:T(8,128)S(1)} %get-tuple-element.818, (s32[]{:T(128)}, f32[7,256,256]{2,1,0:T(8,128)}, f32[7,256,256]{2,1,0:T(8,128)S(1)}, f32[]{:T(128)}, s32[7]{0:T(128)S(1)}, /*index=5*/s32[8,15,256]{2,1,0:T(8,128)S(1)}, f32[7]{0:T(128)S(1)}, ...), branch_computations={%region_15.15_spmd, %region_16.19_spmd} | conditional | flops 139329280 | bytes 5297766 | solution.py:99
  196.8 7.2 %conditional.5 = (f32[256,512]{1,0:T(8,128)S(1)}) conditional(s32[]{:T(128)} %bitcast.85, f32[256,512]{1,0:T(8,128)S(1)} %get-tuple-element.818, (s32[]{:T(128)}, f32[7,256,256]{2,1,0:T(8,128)}, f32[7,256,256]{2,1,0:T(8,128)S(1)}, f32[]{:T(128)}, s32[7]{0:T(128)S(1)}, /*index=5*/s32[8,15,256]{2,1,0:T(8,128)S(1)}, f32[7]{0:T(128)S(1)}, ...), branch_computations={%region_15.15_spmd, %region_16.19_spmd} | conditional | flops 139329280 | bytes 5297766 | solution.py:99
  205.2 7.2 %conditional.5 = (f32[256,512]{1,0:T(8,128)S(1)}) conditional(s32[]{:T(128)} %bitcast.85, f32[256,512]{1,0:T(8,128)S(1)} %get-tuple-element.818, (s32[]{:T(128)}, f32[7,256,256]{2,1,0:T(8,128)}, f32[7,256,256]{2,1,0:T(8,128)S(1)}, f32[]{:T(128)}, s32[7]{0:T(128)S(1)}, /*index=5*/s32[8,15,256]{2,1,0:T(8,128)S(1)}, f32[7]{0:T(128)S(1)}, ...), branch_computations={%region_15.15_spmd, %region_16.19_spmd} | conditional | flops 139329280 | bytes 5297766 | solution.py:99
  213.7 7.2 %conditional.5 = (f32[256,512]{1,0:T(8,128)S(1)}) conditional(s32[]{:T(128)} %bitcast.85, f32[256,512]{1,0:T(8,128)S(1)} %get-tuple-element.818, (s32[]{:T(128)}, f32[7,256,256]{2,1,0:T(8,128)}, f32[7,256,256]{2,1,0:T(8,128)S(1)}, f32[]{:T(128)}, s32[7]{0:T(128)S(1)}, /*index=5*/s32[8,15,256]{2,1,0:T(8,128)S(1)}, f32[7]{0:T(128)S(1)}, ...), branch_computations={%region_15.15_spmd, %region_16.19_spmd} | conditional | flops 139329280 | bytes 5297766 | solution.py:99
  222.2 7.2 %conditional.5 = (f32[256,512]{1,0:T(8,128)S(1)}) conditional(s32[]{:T(128)} %bitcast.85, f32[256,512]{1,0:T(8,128)S(1)} %get-tuple-element.818, (s32[]{:T(128)}, f32[7,256,256]{2,1,0:T(8,128)}, f32[7,256,256]{2,1,0:T(8,128)S(1)}, f32[]{:T(128)}, s32[7]{0:T(128)S(1)}, /*index=5*/s32[8,15,256]{2,1,0:T(8,128)S(1)}, f32[7]{0:T(128)S(1)}, ...), branch_computations={%region_15.15_spmd, %region_16.19_spmd} | conditional | flops 139329280 | bytes 5297766 | solution.py:99
  230.6 7.2 %conditional.5 = (f32[256,512]{1,0:T(8,128)S(1)}) conditional(s32[]{:T(128)} %bitcast.85, f32[256,512]{1,0:T(8,128)S(1)} %get-tuple-element.818, (s32[]{:T(128)}, f32[7,256,256]{2,1,0:T(8,128)}, f32[7,256,256]{2,1,0:T(8,128)S(1)}, f32[]{:T(128)}, s32[7]{0:T(128)S(1)}, /*index=5*/s32[8,15,256]{2,1,0:T(8,128)S(1)}, f32[7]{0:T(128)S(1)}, ...), branch_computations={%region_15.15_spmd, %region_16.19_spmd} | conditional | flops 139329280 | bytes 5297766 | solution.py:99
  (145 shorter events, 108.9 us)
Async XLA Ops:
  7.2 10.9 %copy-start.2 = (bf16[256,512]{1,0:T(8,128)(2,1)S(1)}, bf16[256,512]{1,0:T(8,128)(2,1)}, u32[]{:S(2)}) copy-start(bf16[256,512]{1,0:T(8,128)(2,1)} %param.12) | copy-start | bytes 786436
  7.2 11.0 %copy-start.4 = (s32[1,7]{1,0:T(1,128)S(1)}, s32[1,7]{1,0:T(1,128)}, u32[]{:S(2)}) copy-start(s32[1,7]{1,0:T(1,128)} %param.14) | copy-start | bytes 88
  7.2 54.8 %all-gather.2.cloned.1.call-start = ((), (), s32[]{:S(2)}) async-start(), calls=%async_computation.1 | async-start | bytes 2359296 | tf_op jit(solution)/shard_map/all_gather | solution.py:28
  9.8 168.7 %all-to-all-start = ((s32[8,15,256]{2,1,0:T(8,128)}), s32[8,15,256]{2,1,0:T(8,128)S(1)}, u32[]{:S(2)}, u32[]{:S(2)}) async-start(s32[8,15,256]{2,1,0:T(8,128)} %copy.16), calls=%async_computation | async-start | bytes 262144 | tf_op jit(solution)/shard_map/all_to_all | solution.py:79
  62.0 1.6 copy-start.3
  143.6 33.1 %copy-start.1 = (f32[7,256,256]{1,2,0:T(8,128)}, f32[7,256,256]{1,2,0:T(8,128)S(1)}, u32[]{:S(2)}) copy-start(f32[7,256,256]{1,2,0:T(8,128)S(1)} %get-tuple-element.528) | copy-start | bytes 5505028
  237.8 0.8 copy-start
Sparse Core Ops, SparseCore 0:
  10.1 51.8 all-gather.1
